TPU v7x, 32 devices: a whole 2x2x4 slice. The times are simulated.
32 devices in a mesh: layer: 8 (over y, x, core), dp: 4 (over z).
Axes of the slice: x: 2, y: 2, z: 4, core: 2. Of those that a mesh axis runs over, the one named last changes fastest.
Arguments:
- resid_in: bfloat16 [4, 128, 3584], P(None, 'dp'), may hold values from -6 to 6
- resid_out: bfloat16 [4, 128, 3584], P(None, ('layer', 'dp')), may hold values from -4 to 4
- encoder: bfloat16 [2, 3584, 32768], P(None, None, ('layer', 'dp')), may hold values from -0.09375 to 0.09375
- enc_bias: float32 [2, 32768], P(None, ('layer', 'dp')), may hold values from -3 to 3
- decoder: bfloat16 [5, 32768, 3584], P(None, ('layer', 'dp')), may hold values from -0.046875 to 0.046875
- active: int32 [4, 4, 32], replicated, may hold values from 0 to 127, all different within a row
Outputs:
- recon: bfloat16 [4, 128, 3584], P(None, ('layer', 'dp'))
- grad_encoder: bfloat16 [2, 3584, 32768], P(None, None, ('layer', 'dp'))
- grad_bias: float32 [2, 32768], P(None, ('layer', 'dp'))
- grad_decoder: bfloat16 [5, 32768, 3584], P(None, ('layer', 'dp'))
Inputs may be any that keep to these rules, and one draw needn't show every extreme that they name: Row active[l, n] lists 32 different blocks of layer l, active for tokens n * 32 to (n + 1) * 32 - 1; every block number appears in at least one row of active, counting the rows of all layers together (not necessarily in a row of every layer).
All inputs are finite; a program needn't handle non-finite values.
Results may differ from a plain program's by a relative error of at most 0.0059.
Values may be sent and summed in bfloat16 or wider, within the bound.
A program may use at most 192 MiB of HBM per device.

v0:
```python
import jax
import jax.numpy as jnp
from jax import lax
from jax.sharding import PartitionSpec as P

FEAT = 16384
BLOCK = 128
LAYERS = 4


def per_device(resid_in, resid_out, encoder, enc_bias, decoder, active):
    tok_dev = resid_in.shape[1]
    model_width = resid_in.shape[2]
    local_width = encoder.shape[2]
    dp_count = lax.axis_size("dp")
    all_count = lax.axis_size("layer") * dp_count
    device_rank = lax.axis_index("layer") * dp_count + lax.axis_index("dp")
    first_column = device_rank * local_width
    fold_side = first_column // FEAT
    offset = first_column - fold_side * FEAT
    targets = lax.all_gather(resid_out, ("layer", "dp"), axis=1, tiled=True)
    layer_ids = [fold_side, LAYERS - 1 - fold_side]
    picked = jnp.stack(
        [lax.dynamic_index_in_dim(resid_in, layer_id, 0, keepdims=False) for layer_id in layer_ids]
    )
    inputs = lax.all_gather(picked, "dp", axis=1, tiled=True)
    tokens = inputs.shape[1]
    pre_acts = (
        jnp.einsum("krd,kdf->krf", inputs, encoder, preferred_element_type=jnp.float32)
        + enc_bias[:, None, :]
    )
    block_ids = offset // BLOCK + jnp.arange(local_width // BLOCK, dtype=jnp.int32)
    block_masks = []
    for layer_id in layer_ids:
        listed = lax.dynamic_index_in_dim(active, layer_id, 0, keepdims=False)
        listed_hit = jnp.any(listed[:, :, None] == block_ids[None, None, :], axis=1).astype(
            jnp.float32
        )
        spread = jnp.broadcast_to(
            listed_hit[:, None, :, None], (listed_hit.shape[0], tok_dev, listed_hit.shape[1], BLOCK)
        )
        block_masks.append(spread.reshape(tokens, local_width))
    block_keep = jnp.stack(block_masks)
    positive = jnp.maximum(pre_acts, 0.0)
    feature_codes = (block_keep * positive * positive).astype(jnp.bfloat16)
    pair_table = []
    for pair_slot in range(decoder.shape[0]):
        second = pair_slot >= LAYERS - fold_side
        pair_table.append(
            (second.astype(jnp.int32), jnp.where(second, pair_slot - 1, fold_side + pair_slot))
        )
    decoded = jnp.zeros((LAYERS, tokens, model_width), jnp.float32)
    for pair_slot in range(decoder.shape[0]):
        source_slot, target_layer = pair_table[pair_slot]
        source_codes = lax.dynamic_index_in_dim(feature_codes, source_slot, 0, keepdims=False)
        decoded_part = jnp.dot(source_codes, decoder[pair_slot], preferred_element_type=jnp.float32)
        current = lax.dynamic_index_in_dim(decoded, target_layer, 0, keepdims=False)
        decoded = lax.dynamic_update_index_in_dim(decoded, current + decoded_part, target_layer, 0)
    totals = lax.psum(decoded, ("layer", "dp"))
    share = tokens // all_count
    recon = lax.dynamic_slice_in_dim(totals, device_rank * share, share, 1).astype(jnp.bfloat16)
    errors_all = (totals - targets.astype(jnp.float32)).astype(jnp.bfloat16)
    grad_parts = []
    back_codes = jnp.zeros((2, tokens, local_width), jnp.float32)
    for pair_slot in range(decoder.shape[0]):
        source_slot, target_layer = pair_table[pair_slot]
        source_codes = lax.dynamic_index_in_dim(feature_codes, source_slot, 0, keepdims=False)
        target_errors = lax.dynamic_index_in_dim(errors_all, target_layer, 0, keepdims=False)
        grad_parts.append(
            lax.dot_general(
                source_codes,
                target_errors,
                (((0,), (0,)), ((), ())),
                preferred_element_type=jnp.float32,
            ).astype(jnp.bfloat16)
        )
        pulled = lax.dot_general(
            target_errors,
            decoder[pair_slot],
            (((1,), (1,)), ((), ())),
            preferred_element_type=jnp.float32,
        )
        current = lax.dynamic_index_in_dim(back_codes, source_slot, 0, keepdims=False)
        back_codes = lax.dynamic_update_index_in_dim(back_codes, current + pulled, source_slot, 0)
    grad_decoder = jnp.stack(grad_parts)
    back_pre = (back_codes * block_keep * (2.0 * positive)).astype(jnp.bfloat16)
    grad_encoder = jnp.einsum(
        "krd,krf->kdf", inputs, back_pre, preferred_element_type=jnp.float32
    ).astype(jnp.bfloat16)
    grad_bias = jnp.sum(back_pre.astype(jnp.float32), axis=1)
    return (recon, grad_encoder, grad_bias, grad_decoder)


def solution(mesh):
    in_specs = (
        P(None, "dp", None),
        P(None, ("layer", "dp"), None),
        P(None, None, ("layer", "dp")),
        P(None, ("layer", "dp")),
        P(None, ("layer", "dp"), None),
        P(),
    )
    out_specs = (
        P(None, ("layer", "dp"), None),
        P(None, None, ("layer", "dp")),
        P(None, ("layer", "dp")),
        P(None, ("layer", "dp"), None),
    )
    return jax.shard_map(
        per_device, mesh=mesh, in_specs=in_specs, out_specs=out_specs, check_vma=False
    )
```

profile of v0, /device:TPU:0, one launch (start us, length us, event | category | flops | bytes accessed | tf_op | source)
XLA Modules:
  0.0 404.9 jit_solution(1773918791542335406)
XLA Ops:
  7.3 1.1 constant_dynamic-slice_fusion.9
  8.3 0.8 pad_maximum_fusion
  9.3 0.7 fusion.171
  10.9 43.4 %all-gather.3.cloned.1.call-done = bf16[2,128,3584]{2,1,0:T(8,128)(2,1)} async-done(((bf16[2,32,3584]{2,1,0:T(8,128)(2,1)}), bf16[2,128,3584]{2,1,0:T(8,128)(2,1)}) %all-gather.3.cloned.1.call-update) | async-done | bytes 1835024 | tf_op jit(solution)/shard_map/all_gather | solution.py:26
  54.2 8.0 %fusion.115 = (bf16[2,128,1024]{2,1,0:T(8,128)(2,1)S(1)}, f32[2,128,1024]{2,1,0:T(8,128)S(1)}) fusion(f32[2,128,1024]{2,1,0:T(8,128)S(1)} %constant_dynamic-update-slice_fusion, f32[2,1024]{1,0:T(2,128)S(1)} %copy-done.2, bf16[2,128,3584]{2,1,0:T(8,128)(2,1)} %all-gather.3.cloned.1.call-done, bf16[2,3584,1024]{2,1,0:T(8,128)(2,1)} %param.8), kind=kOutput, calls=%fused_computation.73 | convolution fusion | flops 1880358912 | bytes 19144704 | tf_op jit(solution)/shard_map/krd,kdf->krf/dot_general | solution.py:29
  62.2 3.9 broadcast_in_dim.52
  66.1 5.4 %fusion.33 = f32[4,128,3584]{2,1,0:T(8,128)} fusion(f32[4,128,3584]{2,1,0:T(8,128)} %broadcast_in_dim.52, s32[]{:T(128)S(6)} %select_n.104, bf16[5,1024,3584]{2,1,0:T(8,128)(2,1)} %param.10, bf16[2,128,1024]{2,1,0:T(8,128)(2,1)S(1)} %get-tuple-element.16, s32[]{:T(128)S(6)} %select_n.102), kind=kOutput, calls=%fused_computation.43 | convolution fusion | flops 939524096 | bytes 9437192 | tf_op jit(solution)/shard_map/dot_general | solution.py:56
  71.6 1.6 constant_dynamic-slice_fusion.7
  73.2 5.5 %fusion.42 = f32[4,128,3584]{2,1,0:T(8,128)} fusion(f32[4,128,3584]{2,1,0:T(8,128)} %fusion.33, s32[]{:T(128)S(6)} %select_n.106, bf16[5,1024,3584]{2,1,0:T(8,128)(2,1)} %param.10, f32[1,128,3584]{2,1,0:T(8,128)S(1)} %constant_dynamic-slice_fusion.7, bf16[2,128,1024]{2,1,0:T(8,128)(2,1)S(1)} %get-tuple-element.16, s32[]{:T(128)S(6)} %select_n.107), kind=kOutput, calls=%fused_computation.46 | convolution fusion | flops 939982848 | bytes 11272200 | tf_op jit(solution)/shard_map/dot_general | solution.py:56
  78.7 1.6 constant_dynamic-slice_fusion.6
  80.3 5.5 %fusion.51 = f32[4,128,3584]{2,1,0:T(8,128)} fusion(f32[4,128,3584]{2,1,0:T(8,128)} %fusion.42, s32[]{:T(128)S(6)} %select_n.109, bf16[5,1024,3584]{2,1,0:T(8,128)(2,1)} %param.10, f32[1,128,3584]{2,1,0:T(8,128)S(1)} %constant_dynamic-slice_fusion.6, bf16[2,128,1024]{2,1,0:T(8,128)(2,1)S(1)} %get-tuple-element.16, s32[]{:T(128)S(6)} %select_n.110), kind=kOutput, calls=%fused_computation.49 | convolution fusion | flops 939982848 | bytes 11272200 | tf_op jit(solution)/shard_map/dot_general | solution.py:56
  85.8 1.6 constant_dynamic-slice_fusion.4
  87.4 5.5 %fusion.60 = f32[4,128,3584]{2,1,0:T(8,128)} fusion(f32[4,128,3584]{2,1,0:T(8,128)} %fusion.51, s32[]{:T(128)S(6)} %select_n.112, bf16[5,1024,3584]{2,1,0:T(8,128)(2,1)} %param.10, f32[1,128,3584]{2,1,0:T(8,128)S(1)} %constant_dynamic-slice_fusion.4, bf16[2,128,1024]{2,1,0:T(8,128)(2,1)S(1)} %get-tuple-element.16, s32[]{:T(128)S(6)} %select_n.113), kind=kOutput, calls=%fused_computation.52 | convolution fusion | flops 939982848 | bytes 11272200 | tf_op jit(solution)/shard_map/dot_general | solution.py:56
  92.9 1.6 constant_dynamic-slice_fusion.3
  94.5 5.5 %fusion.69 = f32[4,128,3584]{2,1,0:T(8,128)} fusion(f32[4,128,3584]{2,1,0:T(8,128)} %fusion.60, s32[]{:T(128)S(6)} %select_n.115, bf16[5,1024,3584]{2,1,0:T(8,128)(2,1)} %param.10, f32[1,128,3584]{2,1,0:T(8,128)S(1)} %constant_dynamic-slice_fusion.3, bf16[2,128,1024]{2,1,0:T(8,128)(2,1)S(1)} %get-tuple-element.16, s32[]{:T(128)S(6)} %select_n.116), kind=kOutput, calls=%fused_computation.55 | convolution fusion | flops 939982848 | bytes 11272200 | tf_op jit(solution)/shard_map/dot_general | solution.py:56
  100.3 0.7 copy.19
  101.0 165.3 %all-reduce.2.cloned.1.call-done = f32[4,128,3584]{2,1,0:T(8,128)} async-done(((f32[4,128,3584]{2,1,0:T(8,128)}), f32[4,128,3584]{2,1,0:T(8,128)}) %all-reduce.2.cloned.1.call-update) | async-done | bytes 7340048 | tf_op jit(solution)/shard_map/psum | solution.py:59
  266.3 1.7 dynamic-slice_convert_fusion
  268.0 62.2 %all-gather.5.cloned.1.call-done = bf16[4,128,3584]{2,0,1:T(4,128)(2,1)} async-done(((bf16[4,4,3584]{2,0,1:T(4,128)(2,1)}), bf16[4,128,3584]{2,0,1:T(4,128)(2,1)}) %all-gather.5.cloned.1.call-update) | async-done | bytes 3670032 | tf_op jit(solution)/shard_map/all_gather | solution.py:21
  330.3 5.5 %subtract_convert_fusion = bf16[4,128,3584]{2,1,0:T(8,128)(2,1)S(1)} fusion(f32[4,128,3584]{2,1,0:T(8,128)} %all-reduce.2.cloned.1.call-done, bf16[4,128,3584]{2,0,1:T(4,128)(2,1)} %all-gather.5.cloned.1.call-done), kind=kLoop, calls=%fused_computation.31 | loop fusion | flops 5505024 | bytes 14680064 | tf_op jit(solution)/shard_map/convert_element_type | solution.py:62
  335.7 5.2 %bitcast_dynamic-update-slice_fusion.4 = bf16[5,1024,3584]{2,1,0:T(8,128)(2,1)} fusion(bf16[4,128,3584]{2,1,0:T(8,128)(2,1)S(1)} %subtract_convert_fusion, s32[]{:T(128)S(6)} %select_n.104, bf16[2,128,1024]{2,1,0:T(8,128)(2,1)S(1)} %get-tuple-element.16, s32[]{:T(128)S(6)} %select_n.102), kind=kOutput, calls=%fused_computation.10 | convolution fusion | flops 943194112 | bytes 8519688 | tf_op jit(solution)/shard_map/dot_general | solution.py:70
  340.9 5.1 %bitcast_dynamic-update-slice_fusion.3 = bf16[5,1024,3584]{2,1,0:T(8,128)(2,1)} fusion(bf16[5,1024,3584]{2,1,0:T(8,128)(2,1)} %bitcast_dynamic-update-slice_fusion.4, bf16[4,128,3584]{2,1,0:T(8,128)(2,1)S(1)} %subtract_convert_fusion, s32[]{:T(128)S(6)} %select_n.106, bf16[2,128,1024]{2,1,0:T(8,128)(2,1)S(1)} %get-tuple-element.16, s32[]{:T(128)S(6)} %select_n.107), kind=kOutput, calls=%fused_computation.9 | convolution fusion | flops 943194112 | bytes 8519688 | tf_op jit(solution)/shard_map/dot_general | solution.py:70
  346.0 5.1 %bitcast_dynamic-update-slice_fusion.2 = bf16[5,1024,3584]{2,1,0:T(8,128)(2,1)} fusion(bf16[5,1024,3584]{2,1,0:T(8,128)(2,1)} %bitcast_dynamic-update-slice_fusion.3, bf16[4,128,3584]{2,1,0:T(8,128)(2,1)S(1)} %subtract_convert_fusion, s32[]{:T(128)S(6)} %select_n.109, bf16[2,128,1024]{2,1,0:T(8,128)(2,1)S(1)} %get-tuple-element.16, s32[]{:T(128)S(6)} %select_n.110), kind=kOutput, calls=%fused_computation.8 | convolution fusion | flops 943194112 | bytes 8519688 | tf_op jit(solution)/shard_map/dot_general | solution.py:70
  351.2 5.1 %bitcast_dynamic-update-slice_fusion.1 = bf16[5,1024,3584]{2,1,0:T(8,128)(2,1)} fusion(bf16[5,1024,3584]{2,1,0:T(8,128)(2,1)} %bitcast_dynamic-update-slice_fusion.2, bf16[4,128,3584]{2,1,0:T(8,128)(2,1)S(1)} %subtract_convert_fusion, s32[]{:T(128)S(6)} %select_n.112, bf16[2,128,1024]{2,1,0:T(8,128)(2,1)S(1)} %get-tuple-element.16, s32[]{:T(128)S(6)} %select_n.113), kind=kOutput, calls=%fused_computation.7 | convolution fusion | flops 943194112 | bytes 8519688 | tf_op jit(solution)/shard_map/dot_general | solution.py:70
  356.3 5.1 %bitcast_dynamic-update-slice_fusion = bf16[5,1024,3584]{2,1,0:T(8,128)(2,1)} fusion(bf16[5,1024,3584]{2,1,0:T(8,128)(2,1)} %bitcast_dynamic-update-slice_fusion.1, bf16[4,128,3584]{2,1,0:T(8,128)(2,1)S(1)} %subtract_convert_fusion, s32[]{:T(128)S(6)} %select_n.115, bf16[2,128,1024]{2,1,0:T(8,128)(2,1)S(1)} %get-tuple-element.16, s32[]{:T(128)S(6)} %select_n.116), kind=kOutput, calls=%fused_computation.6 | convolution fusion | flops 943194112 | bytes 8519688 | tf_op jit(solution)/shard_map/dot_general | solution.py:70
  361.6 5.7 %fusion.76 = f32[2,128,1024]{2,1,0:T(8,128)S(1)} fusion(f32[2,128,1024]{2,1,0:T(8,128)S(1)} %broadcast.16, s32[]{:T(128)S(6)} %select_n.102, bf16[5,1024,3584]{2,1,0:T(8,128)(2,1)} %param.10, bf16[4,128,3584]{2,1,0:T(8,128)(2,1)S(1)} %subtract_convert_fusion, s32[]{:T(128)S(6)} %select_n.104), kind=kOutput, calls=%fused_computation.60 | convolution fusion | flops 939524096 | bytes 8781832 | tf_op jit(solution)/shard_map/dot_general | solution.py:77
  367.4 5.5 %fusion.85 = f32[2,128,1024]{2,1,0:T(8,128)S(1)} fusion(f32[2,128,1024]{2,1,0:T(8,128)S(1)} %fusion.76, s32[]{:T(128)S(6)} %select_n.107, bf16[5,1024,3584]{2,1,0:T(8,128)(2,1)} %param.10, bf16[4,128,3584]{2,1,0:T(8,128)(2,1)S(1)} %subtract_convert_fusion, s32[]{:T(128)S(6)} %select_n.106, f32[1,128,1024]{2,1,0:T(8,128)S(1)} %constant_dynamic-slice_fusion.2), kind=kOutput, calls=%fused_computation.63 | convolution fusion | flops 939655168 | bytes 9306120 | tf_op jit(solution)/shard_map/dot_general | solution.py:77
  373.0 5.5 %fusion.94 = f32[2,128,1024]{2,1,0:T(8,128)S(1)} fusion(f32[2,128,1024]{2,1,0:T(8,128)S(1)} %fusion.85, s32[]{:T(128)S(6)} %select_n.110, bf16[5,1024,3584]{2,1,0:T(8,128)(2,1)} %param.10, bf16[4,128,3584]{2,1,0:T(8,128)(2,1)S(1)} %subtract_convert_fusion, s32[]{:T(128)S(6)} %select_n.109, f32[1,128,1024]{2,1,0:T(8,128)S(1)} %constant_dynamic-slice_fusion.1), kind=kOutput, calls=%fused_computation.66 | convolution fusion | flops 939655168 | bytes 9306120 | tf_op jit(solution)/shard_map/dot_general | solution.py:77
  378.6 5.5 %fusion.103 = f32[2,128,1024]{2,1,0:T(8,128)S(1)} fusion(f32[2,128,1024]{2,1,0:T(8,128)S(1)} %fusion.94, s32[]{:T(128)S(6)} %select_n.113, bf16[5,1024,3584]{2,1,0:T(8,128)(2,1)} %param.10, bf16[4,128,3584]{2,1,0:T(8,128)(2,1)S(1)} %subtract_convert_fusion, s32[]{:T(128)S(6)} %select_n.112, f32[1,128,1024]{2,1,0:T(8,128)S(1)} %constant_dynamic-slice_fusion), kind=kOutput, calls=%fused_computation.69 | convolution fusion | flops 939655168 | bytes 9306120 | tf_op jit(solution)/shard_map/dot_general | solution.py:77
  384.2 5.7 %fusion.112 = f32[2,128,1024]{2,1,0:T(8,128)S(1)} fusion(f32[2,128,1024]{2,1,0:T(8,128)S(1)} %fusion.103, s32[]{:T(128)S(6)} %select_n.116, bf16[5,1024,3584]{2,1,0:T(8,128)(2,1)} %param.10, bf16[4,128,3584]{2,1,0:T(8,128)(2,1)S(1)} %subtract_convert_fusion, s32[]{:T(128)S(6)} %select_n.115, f32[1,128,1024]{2,1,0:T(8,128)S(1)} %constant_dynamic-slice_fusion.5), kind=kOutput, calls=%fused_computation.72 | convolution fusion | flops 939655168 | bytes 9306120 | tf_op jit(solution)/shard_map/dot_general | solution.py:77
  389.9 1.0 convert_reduce_fusion
  390.8 7.6 %convolution_convert_fusion = bf16[2,3584,1024]{2,1,0:T(8,128)(2,1)} fusion(bf16[2,128,3584]{2,1,0:T(8,128)(2,1)S(1)} %copy-done, bf16[2,128,1024]{2,1,0:T(8,128)(2,1)S(1)} %get-tuple-element.11), kind=kOutput, calls=%fused_computation | convolution fusion | flops 1886388224 | bytes 17039360 | tf_op jit(solution)/shard_map/krd,krf->kdf/dot_general | solution.py:87
  (27 shorter events, 1.4 us)
Async XLA Ops:
  7.2 47.1 %copy-start.2 = (f32[2,1024]{1,0:T(2,128)S(1)}, f32[2,1024]{1,0:T(2,128)}, u32[]{:S(2)}) copy-start(f32[2,1024]{1,0:T(2,128)} %param.9) | copy-start | bytes 24580
  7.2 47.0 %all-gather.3.cloned.1.call-start = ((), (), s32[]{:S(2)}) async-start(), calls=%async_computation | async-start | bytes 2293760 | tf_op jit(solution)/shard_map/all_gather | solution.py:26
  9.2 257.1 %all-reduce.2.cloned.1.call-start = ((), (), s32[]{:S(2)}) async-start(), calls=%async_computation.1 | async-start | bytes 14680064 | tf_op jit(solution)/shard_map/psum | solution.py:59
  94.5 5.8 %copy-start.1 = (bf16[4,4,3584]{2,1,0:T(4,128)(2,1)S(1)}, bf16[4,4,3584]{2,1,0:T(4,128)(2,1)}, u32[]{:S(2)}) copy-start(bf16[4,4,3584]{2,1,0:T(4,128)(2,1)} %param.7) | copy-start | bytes 344068
  100.0 230.2 %all-gather.5.cloned.1.call-start = ((), (), s32[]{:S(2)}) async-start(), calls=%async_computation.2 | async-start | bytes 3784704 | tf_op jit(solution)/shard_map/all_gather | solution.py:21
  384.2 6.6 %copy-start = (bf16[2,128,3584]{2,1,0:T(8,128)(2,1)S(1)}, bf16[2,128,3584]{2,1,0:T(8,128)(2,1)}, u32[]{:S(2)}) copy-start(bf16[2,128,3584]{2,1,0:T(8,128)(2,1)} %all-gather.3.cloned.1.call-done) | copy-start | bytes 5505028
Sparse Core Ops, SparseCore 0:
  10.1 44.0 all-gather.2
  100.2 166.0 all-reduce.1
  269.7 60.4 all-gather.4
where the time goes:
time: 406 us; the launch traced here: 405 us
  waiting for transfers between devices  271 us (67%)
  matrix products  96.6 us (24%)
  local copies, waits for them, and re-layouts  15.4 us (4%)
  between operations  14.1 us (3%)
  other arithmetic  7.55 us (2%)
    psum x1, waiting for transfers between devices, per_device(): totals = lax.psum(decoded, ('layer', 'dp'))  165 us
    all_gather x1, waiting for transfers between devices, per_device(): targets = lax.all_gather(resid_out, ('layer', 'dp'), axis=1, tiled=True)  62.2 us
    all_gather x1, waiting for transfers between devices, per_device(): inputs = lax.all_gather(picked, 'dp', axis=1, tiled=True)  43.4 us
    dot_general x5, matrix products, per_device(): lax.dot_general(target_errors, decoder[pair_slot], (((1,), (1,)), ((), ()...  28 us
    dot_general x5, matrix products, per_device(): jnp.dot(source_codes, decoder[pair_slot], preferred_element_type=jnp.floa...  27.3 us
    dot_general x5, matrix products, per_device(): lax.dot_general(source_codes, target_errors, (((0,), (0,)), ((), ())), pr...  25.7 us
  transfers between devices with their start and end apart: 3, of which 3 were waited for; matrix products, arithmetic and copies ran while one was open for 1% of the time, Pallas kernels for 0%

commit v1 on v0

--- a/solution.py
+++ b/solution.py
@@ -56,7 +56,8 @@
         decoded_part = jnp.dot(source_codes, decoder[pair_slot], preferred_element_type=jnp.float32)
         current = lax.dynamic_index_in_dim(decoded, target_layer, 0, keepdims=False)
         decoded = lax.dynamic_update_index_in_dim(decoded, current + decoded_part, target_layer, 0)
-    totals = lax.psum(decoded, ("layer", "dp"))
+    upper = lax.psum(decoded, "dp")
+    totals = lax.psum(upper, "layer")
     share = tokens // all_count
     recon = lax.dynamic_slice_in_dim(totals, device_rank * share, share, 1).astype(jnp.bfloat16)
     errors_all = (totals - targets.astype(jnp.float32)).astype(jnp.bfloat16)

time: 406 us -> 559 us (1.38)
  waiting for transfers between devices: 271 us -> 423 us
    psum x1 -> x2, waiting for transfers between devices: 165 us -> 368 us  [the longest x1 261 us: per_device(): upper = lax.psum(decoded, 'dp')]
    all_gather x1, waiting for transfers between devices: 62.2 us -> 11.6 us  [per_device(): targets = lax.all_gather(resid_out, ('layer', 'dp'), axis=1, tiled=True)]
  transfers between devices with their start and end apart: 3 -> 4, of which waited for: 3 -> 4; matrix products, arithmetic and copies ran while one was open for 1% -> 0% of each run, Pallas kernels for 0% -> 0%
where the time goes in v1:
time: 559 us; the launch traced here: 558 us
  waiting for transfers between devices  423 us (76%)
  matrix products  96.6 us (17%)
  between operations  15.5 us (3%)
  local copies, waits for them, and re-layouts  15.4 us (3%)
  other arithmetic  7.55 us (1%)
    psum x1, waiting for transfers between devices, per_device(): upper = lax.psum(decoded, 'dp')  261 us
    psum x1, waiting for transfers between devices, per_device(): totals = lax.psum(upper, 'layer')  107 us
    all_gather x1, waiting for transfers between devices, per_device(): inputs = lax.all_gather(picked, 'dp', axis=1, tiled=True)  43.4 us
    dot_general x5, matrix products, per_device(): lax.dot_general(target_errors, decoder[pair_slot], (((1,), (1,)), ((), ()...  28 us
    dot_general x5, matrix products, per_device(): jnp.dot(source_codes, decoder[pair_slot], preferred_element_type=jnp.floa...  27.3 us
    dot_general x5, matrix products, per_device(): lax.dot_general(source_codes, target_errors, (((0,), (0,)), ((), ())), pr...  25.7 us
    all_gather x1, waiting for transfers between devices, per_device(): targets = lax.all_gather(resid_out, ('layer', 'dp'), axis=1, tiled=True)  11.6 us
  transfers between devices with their start and end apart: 4, of which 4 were waited for; matrix products, arithmetic and copies ran while one was open for 0% of the time, Pallas kernels for 0%

profile of v1, /device:TPU:0, one launch (start us, length us, event | category | flops | bytes accessed | tf_op | source)
XLA Modules:
  0.0 558.3 jit_solution(5332202097280985552)
XLA Ops:
  8.1 1.1 constant_dynamic-slice_fusion.9
  9.2 0.8 pad_maximum_fusion
  10.1 0.7 fusion.171
  11.7 43.4 %all-gather.3.cloned.1.call-done = bf16[2,128,3584]{2,1,0:T(8,128)(2,1)} async-done(((bf16[2,32,3584]{2,1,0:T(8,128)(2,1)}), bf16[2,128,3584]{2,1,0:T(8,128)(2,1)}) %all-gather.3.cloned.1.call-update) | async-done | bytes 1835024 | tf_op jit(solution)/shard_map/all_gather | solution.py:26
  55.1 8.0 %fusion.115 = (bf16[2,128,1024]{2,1,0:T(8,128)(2,1)S(1)}, f32[2,128,1024]{2,1,0:T(8,128)S(1)}) fusion(f32[2,128,1024]{2,1,0:T(8,128)S(1)} %constant_dynamic-update-slice_fusion, f32[2,1024]{1,0:T(2,128)S(1)} %copy-done.2, bf16[2,128,3584]{2,1,0:T(8,128)(2,1)} %all-gather.3.cloned.1.call-done, bf16[2,3584,1024]{2,1,0:T(8,128)(2,1)} %param.8), kind=kOutput, calls=%fused_computation.73 | convolution fusion | flops 1880358912 | bytes 19144704 | tf_op jit(solution)/shard_map/krd,kdf->krf/dot_general | solution.py:29
  63.0 3.9 broadcast_in_dim.52
  67.0 5.4 fusion.33
  72.4 1.6 constant_dynamic-slice_fusion.7
  74.0 5.5 fusion.42
  79.5 1.6 constant_dynamic-slice_fusion.6
  81.1 5.5 fusion.51
  86.6 1.6 constant_dynamic-slice_fusion.4
  88.2 5.5 fusion.60
  93.7 1.6 constant_dynamic-slice_fusion.3
  95.4 5.5 fusion.69
  101.9 260.7 %all-reduce.3.cloned.1.call-done = f32[4,128,3584]{2,1,0:T(8,128)} async-done(((f32[4,128,3584]{2,1,0:T(8,128)}), f32[4,128,3584]{2,1,0:T(8,128)}) %all-reduce.3.cloned.1.call-update) | async-done | bytes 7340048 | tf_op jit(solution)/shard_map/psum | solution.py:59
  362.7 11.6 %all-gather.5.cloned.1.call-done = bf16[4,128,3584]{2,0,1:T(4,128)(2,1)} async-done(((bf16[4,4,3584]{2,0,1:T(4,128)(2,1)}), bf16[4,128,3584]{2,0,1:T(4,128)(2,1)}) %all-gather.5.cloned.1.call-update) | async-done | bytes 3670032 | tf_op jit(solution)/shard_map/all_gather | solution.py:21
  374.2 107.1 %all-reduce.5.cloned.1.call-done = f32[4,128,3584]{2,1,0:T(8,128)} async-done(((f32[4,128,3584]{2,1,0:T(8,128)}), f32[4,128,3584]{2,1,0:T(8,128)}) %all-reduce.5.cloned.1.call-update) | async-done | bytes 7340048 | tf_op jit(solution)/shard_map/psum | solution.py:60
  481.3 5.5 subtract_convert_fusion
  486.8 5.2 bitcast_dynamic-update-slice_fusion.4
  491.9 5.1 bitcast_dynamic-update-slice_fusion.3
  497.1 5.1 bitcast_dynamic-update-slice_fusion.2
  502.2 5.1 bitcast_dynamic-update-slice_fusion.1
  507.4 5.1 bitcast_dynamic-update-slice_fusion
  512.6 5.5 fusion.76
  518.2 5.7 %fusion.85 = f32[2,128,1024]{2,1,0:T(8,128)S(1)} fusion(f32[2,128,1024]{2,1,0:T(8,128)S(1)} %fusion.76, s32[]{:T(128)S(6)} %select_n.107, bf16[5,1024,3584]{2,1,0:T(8,128)(2,1)} %param.10, bf16[4,128,3584]{2,1,0:T(8,128)(2,1)S(1)} %subtract_convert_fusion, s32[]{:T(128)S(6)} %select_n.106, f32[1,128,1024]{2,1,0:T(8,128)S(1)} %constant_dynamic-slice_fusion.2), kind=kOutput, calls=%fused_computation.63 | convolution fusion | flops 939655168 | bytes 9306120 | tf_op jit(solution)/shard_map/dot_general | solution.py:78
  524.0 5.5 fusion.94
  529.6 5.5 fusion.103
  535.2 5.7 %fusion.112 = f32[2,128,1024]{2,1,0:T(8,128)S(1)} fusion(f32[2,128,1024]{2,1,0:T(8,128)S(1)} %fusion.103, s32[]{:T(128)S(6)} %select_n.116, bf16[5,1024,3584]{2,1,0:T(8,128)(2,1)} %param.10, bf16[4,128,3584]{2,1,0:T(8,128)(2,1)S(1)} %subtract_convert_fusion, s32[]{:T(128)S(6)} %select_n.115, f32[1,128,1024]{2,1,0:T(8,128)S(1)} %constant_dynamic-slice_fusion.5), kind=kOutput, calls=%fused_computation.72 | convolution fusion | flops 939655168 | bytes 9306120 | tf_op jit(solution)/shard_map/dot_general | solution.py:78
  540.9 1.0 convert_reduce_fusion
  541.9 7.6 %convolution_convert_fusion = bf16[2,3584,1024]{2,1,0:T(8,128)(2,1)} fusion(bf16[2,128,3584]{2,1,0:T(8,128)(2,1)S(1)} %copy-done, bf16[2,128,1024]{2,1,0:T(8,128)(2,1)S(1)} %get-tuple-element.11), kind=kOutput, calls=%fused_computation | convolution fusion | flops 1886388224 | bytes 17039360 | tf_op jit(solution)/shard_map/krd,krf->kdf/dot_general | solution.py:88
  549.4 1.7 dynamic-slice_convert_fusion
  (30 shorter events, 2.2 us)
Async XLA Ops:
  8.0 47.1 %copy-start.2 = (f32[2,1024]{1,0:T(2,128)S(1)}, f32[2,1024]{1,0:T(2,128)}, u32[]{:S(2)}) copy-start(f32[2,1024]{1,0:T(2,128)} %param.9) | copy-start | bytes 24580
  8.0 47.0 %all-gather.3.cloned.1.call-start = ((), (), s32[]{:S(2)}) async-start(), calls=%async_computation | async-start | bytes 2293760 | tf_op jit(solution)/shard_map/all_gather | solution.py:26
  10.0 352.6 %all-reduce.3.cloned.1.call-start = ((), (), s32[]{:S(2)}) async-start(), calls=%async_computation.1 | async-start | bytes 14680064 | tf_op jit(solution)/shard_map/psum | solution.py:59
  95.3 5.6 %copy-start.1 = (bf16[4,4,3584]{2,1,0:T(4,128)(2,1)S(1)}, bf16[4,4,3584]{2,1,0:T(4,128)(2,1)}, u32[]{:S(2)}) copy-start(bf16[4,4,3584]{2,1,0:T(4,128)(2,1)} %param.7) | copy-start | bytes 344068
  100.9 273.3 %all-gather.5.cloned.1.call-start = ((), (), s32[]{:S(2)}) async-start(), calls=%async_computation.3 | async-start | bytes 3784704 | tf_op jit(solution)/shard_map/all_gather | solution.py:21
  101.7 379.6 %all-reduce.5.cloned.1.call-start = ((), (), s32[]{:S(2)}) async-start(), calls=%async_computation.2 | async-start | bytes 14680064 | tf_op jit(solution)/shard_map/psum | solution.py:60
  535.2 6.6 %copy-start = (bf16[2,128,3584]{2,1,0:T(8,128)(2,1)S(1)}, bf16[2,128,3584]{2,1,0:T(8,128)(2,1)}, u32[]{:S(2)}) copy-start(bf16[2,128,3584]{2,1,0:T(8,128)(2,1)} %all-gather.3.cloned.1.call-done) | copy-start | bytes 5505028
Sparse Core Ops, SparseCore 0:
  11.0 44.0 all-gather.2
  101.0 261.5 all-reduce.2
  365.9 115.3 all-reduce.4
Sparse Core Ops, SparseCore 1:
  104.8 269.4 all-gather.4
